TPU v7x, 256 devices: a whole 4x4x8 slice. The times are simulated.
256 devices in a mesh: seq: 64 (over x, z, core), tp: 4 (over y).
Axes of the slice: x: 4, y: 4, z: 8, core: 2. Of those that a mesh axis runs over, the one named last changes fastest.
Arguments:
- token_ids: int32 [65536], P('seq'), may hold values from 0 to 511
- embed_table: bfloat16 [512, 2048], P(None, 'tp'), may hold values from -6 to 6
- norm_gain: float32 [2048], replicated, may hold values from 0.1 to 1.9
- in_weight: bfloat16 [2048, 3, 2048], P('seq', None, 'tp'), may hold values from -0.125 to 0.125
- short_filter: float32 [7, 3, 2048], P(None, None, 'tp'), may hold values from -2.4 to 2.4
- long_filter: bfloat16 [128, 128], P('tp'), may hold values from -0.5390625 to 0.5390625
- long_skip: float32 [2048], P('tp'), may hold values from -3 to 3
- out_weight: bfloat16 [2048, 2048], P('tp', 'seq'), may hold values from -0.125 to 0.125
Outputs:
- mixed: bfloat16 [65536, 2048], P('seq', 'tp')
All inputs are finite; a program needn't handle non-finite values.
Results may differ from a plain program's by a relative error of at most 0.012.
Values may be sent and summed in bfloat16 or wider, within the bound.
A program may use at most 64 MiB of HBM per device.

v0:
```python
import jax
import jax.numpy as jnp
from jax import lax
from jax.sharding import PartitionSpec as P


def from_behind(block, axis, distance):
    devices = range(lax.axis_size(axis))
    route = [(i - distance, i) for i in devices if i - distance in devices]
    return lax.ppermute(block, axis, route)


def short_conv(extended, short_filter, out_length):
    short_taps = short_filter.shape[0]
    running = jnp.zeros((out_length,) + extended.shape[1:], jnp.float32)
    for tap_index in range(short_taps):
        begin = short_taps - 1 - tap_index
        running = running + short_filter[tap_index][None] * extended[
            begin : begin + out_length
        ].astype(jnp.float32)
    return running


def body(
    token_ids, embed_table, norm_gain, in_weight, short_filter, long_filter, long_skip, out_weight
):
    tok_count = token_ids.shape[0]
    vocab_size = embed_table.shape[0]
    local_width = embed_table.shape[1]
    onehot = (token_ids[:, None] == jnp.arange(vocab_size, dtype=jnp.int32)[None, :]).astype(
        jnp.bfloat16
    )
    own_feats = jnp.dot(onehot, embed_table, preferred_element_type=jnp.float32).astype(
        jnp.bfloat16
    )
    features = lax.all_gather(own_feats, "tp", axis=1, tiled=True)
    widened = features.astype(jnp.float32)
    scaled = (
        widened
        * lax.rsqrt(jnp.mean(widened * widened, axis=1, keepdims=True) + 1e-06)
        * norm_gain[None, :]
    )
    normed = scaled.astype(jnp.bfloat16)
    projected = jnp.einsum(
        "td,dsc->tsc",
        normed,
        lax.all_gather(in_weight, "seq", axis=0, tiled=True),
        preferred_element_type=jnp.float32,
    ).astype(jnp.bfloat16)
    tap_count = long_filter.shape[1]
    short_taps = short_filter.shape[0]
    rim_rows = from_behind(projected[tok_count - short_taps + 1 :], "seq", 1)
    extended = jnp.concatenate([rim_rows, projected], axis=0)
    featured = short_conv(extended, short_filter, tok_count)
    queries = featured[:, 0]
    gated_kv = (featured[:, 1] * featured[:, 2]).astype(jnp.bfloat16)
    earlier = from_behind(gated_kv[tok_count - tap_count :], "seq", 1)
    product = jnp.concatenate([earlier, gated_kv], axis=0)
    groups_here = long_filter.shape[0]
    group_size = local_width // groups_here
    positions = jnp.arange(tap_count, dtype=jnp.int32)
    differ = positions[:, None, None] - positions[None, :, None]
    target = positions[None, None, :]
    near_pick = (differ == target).astype(jnp.float32)
    far_pick = (differ + tap_count == target).astype(jnp.float32)
    filter_f32 = long_filter.astype(jnp.float32)
    near_band = jnp.einsum("isj,gj->gis", near_pick, filter_f32).astype(jnp.bfloat16)
    far_band = jnp.einsum("isj,gj->gis", far_pick, filter_f32).astype(jnp.bfloat16)
    blocks = product.reshape(tok_count // tap_count + 1, tap_count, groups_here, group_size)
    convolved = jnp.einsum(
        "gis,bsgc->bigc", near_band, blocks[1:], preferred_element_type=jnp.float32
    )
    convolved = convolved + jnp.einsum(
        "gis,bsgc->bigc", far_band, blocks[:-1], preferred_element_type=jnp.float32
    )
    convolved = convolved.reshape(tok_count, local_width) + long_skip[None, :] * product[
        tap_count:
    ].astype(jnp.float32)
    gated = (queries * convolved).astype(jnp.bfloat16)
    partials = jnp.dot(
        gated,
        lax.all_gather(out_weight, "seq", axis=1, tiled=True),
        preferred_element_type=jnp.float32,
    )
    summed = lax.psum(partials.astype(jnp.bfloat16), "tp").astype(jnp.float32)
    own_share = lax.dynamic_slice_in_dim(summed, lax.axis_index("tp") * local_width, local_width, 1)
    return (own_feats.astype(jnp.float32) + own_share).astype(jnp.bfloat16)


def solution(mesh):
    placed = (
        P("seq"),
        P(None, "tp"),
        P(),
        P("seq", None, "tp"),
        P(None, None, "tp"),
        P("tp", None),
        P("tp"),
        P("tp", "seq"),
    )
    return jax.shard_map(
        body, mesh=mesh, in_specs=placed, out_specs=P("seq", "tp"), check_vma=False
    )
```

profile of v0, /device:TPU:1, one launch (start us, length us, event | category | flops | bytes accessed | tf_op | source)
XLA Modules:
  0.0 337.5 jit_solution(16231888260444834584)
XLA Ops:
  6.5 0.0 copy-start
  6.5 0.0 all-gather.4.cloned.1.call-start
  6.5 1.0 copy-done
  7.6 2.4 fusion.24
  10.0 0.0 all-gather.4.cloned.1.call-update
  10.0 0.0 all-gather.6.cloned.1.call-start
  10.1 0.7 all-gather.6.cloned.1.call-update
  10.8 0.0 all-gather.8.cloned.1.call-start
  10.8 0.7 all-gather.8.cloned.1.call-update
  11.5 0.0 all-reduce.2.cloned.1.call-start
  11.6 1.2 fusion.38
  12.8 0.0 copy-start.6
  12.8 5.8 %fusion.3 = bf16[128,128,32]{1,2,0:T(8,128)(2,1)} fusion(s32[128,128]{1,0:T(8,128)S(1)} %iota_subtract_fusion, bf16[32,128]{1,0:T(8,128)(2,1)} %param.13), kind=kOutput, calls=%fused_computation.7 | convolution fusion | flops 136314880 | bytes 1122304 | tf_op jit(solution)/shard_map/isj,gj->gis/dot_general | solution.py:67
  18.6 0.0 copy-done.5
  18.6 5.1 %fusion.4 = bf16[128,128,32]{1,2,0:T(8,128)(2,1)} fusion(s32[128,128]{1,0:T(8,128)S(1)} %broadcast_add_fusion, bf16[32,128]{1,0:T(8,128)(2,1)S(1)} %copy-done.5), kind=kOutput, calls=%fused_computation.8 | convolution fusion | flops 136314880 | bytes 1122304 | tf_op jit(solution)/shard_map/isj,gj->gis/dot_general | solution.py:68
  23.7 40.8 %all-gather.4.cloned.1.call-done = bf16[1024,2048]{1,0:T(8,128)(2,1)} async-done(((bf16[1024,512]{1,0:T(8,128)(2,1)}), bf16[1024,2048]{1,0:T(8,128)(2,1)}) %all-gather.4.cloned.1.call-update) | async-done | bytes 4194320 | tf_op jit(solution)/shard_map/all_gather | solution.py:36
  64.6 3.1 fusion
  67.7 81.2 %all-gather.6.cloned.1.call-done = bf16[2048,3,512]{2,0,1:T(8,128)(2,1)} async-done(((bf16[32,3,512]{2,0,1:T(8,128)(2,1)}), bf16[2048,3,512]{2,0,1:T(8,128)(2,1)}) %all-gather.6.cloned.1.call-update) | async-done | bytes 6291472 | tf_op jit(solution)/shard_map/all_gather | solution.py:47
  148.8 0.0 copy-done.6
  148.8 10.5 %fusion.17 = bf16[1024,3,512]{2,0,1:T(8,128)(2,1)S(1)} fusion(bf16[2048,3,512]{2,0,1:T(8,128)(2,1)} %all-gather.6.cloned.1.call-done, bf16[1024,2048]{1,0:T(8,128)(2,1)} %all-gather.4.cloned.1.call-done, f32[2048]{0:T(1024)S(1)} %copy-done.6, f32[1024]{0:T(1024)S(1)} %add_rsqrt_fusion), kind=kOutput, calls=%fused_computation.31 | convolution fusion | flops 6452412416 | bytes 13643776 | tf_op jit(solution)/shard_map/td,dsc->tsc/dot_general | solution.py:44
  159.4 2.8 collective-permute-start
  162.2 0.9 collective-permute-done
  163.1 5.6 %multiply_add_fusion = f32[1024,3,512]{2,0,1:T(8,128)S(1)} fusion(bf16[1024,3,512]{2,0,1:T(8,128)(2,1)S(1)} %fusion.17, bf16[6,3,512]{2,0,1:T(8,128)(2,1)S(1)} %collective-permute-done, f32[3,512]{1,0:T(4,128)S(1)} %get-tuple-element.12, f32[3,512]{1,0:T(4,128)S(1)} %get-tuple-element.13, f32[3,512]{1,0:T(4,128)S(1)} %get-tuple-element.14, ...), kind=kLoop, calls=%fused_computation.14 | loop fusion | flops 59768832 | bytes 9498624 | tf_op jit(solution)/shard_map/add | solution.py:18
  168.7 0.0 copy-start.1
  168.7 2.7 copy-done.1
  171.3 0.4 fusion.20
  171.7 0.0 copy-start.3
  171.7 0.5 copy.12
  172.2 0.0 copy-start.2
  172.3 4.7 %collective-permute-start.1 = (bf16[128,512]{1,0:T(8,128)(2,1)S(1)}, bf16[128,512]{1,0:T(8,128)(2,1)S(1)}, u32[]{:S(2)}, u32[]{:S(2)}) collective-permute-start(bf16[128,512]{1,0:T(8,128)(2,1)S(1)} %slice_bitcast_fusion.1), channel_id=1, source_target_pairs={{0,4},{4,8},{8,12},{12,16},{16,20},{20,24},{24,28},{28,32},{32,36}... | collective-permute-start | bytes 393224 | tf_op jit(solution)/shard_map/ppermute | solution.py:10
  176.9 0.3 copy.29
  177.2 0.0 copy-done.3
  177.2 2.1 fusion.26
  179.3 0.4 fusion.42
  179.7 0.0 collective-permute-done.1
  179.7 1.1 pad_maximum_fusion.1
  180.7 2.3 copy.14
  183.0 1.5 copy.30
  184.5 2.1 add_bitcast_fusion
  186.6 0.0 copy-start.7
  186.6 0.9 copy.16
  187.5 0.5 copy.52
  188.0 1.8 copy.17
  189.8 35.9 %all-gather.8.cloned.1.call-done = bf16[512,2048]{0,1:T(8,128)(2,1)} async-done(((bf16[512,32]{0,1:T(8,128)(2,1)}), bf16[512,2048]{0,1:T(8,128)(2,1)}) %all-gather.8.cloned.1.call-update) | async-done | bytes 2097168 | tf_op jit(solution)/shard_map/all_gather | solution.py:82
  225.7 7.6 %convolution_convert_fusion = bf16[1024,2048]{1,0:T(8,128)(2,1)} fusion(bf16[512,2048]{0,1:T(8,128)(2,1)} %all-gather.8.cloned.1.call-done, f32[1024,3,512]{2,0,1:T(8,128)} %copy-done.1, f32[1024,512]{1,0:T(8,128)} %copy.17, f32[512]{0:T(512)S(1)} %copy-done.7, bf16[1024,1,512]{2,0,1:T(8,128)(2,1)} %copy-done.3), kind=kOutput, calls=%fused_computation.21 | convolution fusion | flops 2152202240 | bytes 11536384 | tf_op jit(solution)/shard_map/dot_general | solution.py:80
  233.3 0.0 all-reduce.2.cloned.1.call-update
  233.3 95.2 %all-reduce.2.cloned.1.call-done = bf16[1024,2048]{1,0:T(8,128)(2,1)} async-done(((bf16[1024,2048]{1,0:T(8,128)(2,1)}), bf16[1024,2048]{1,0:T(8,128)(2,1)}) %all-reduce.2.cloned.1.call-update) | async-done | bytes 4194320 | tf_op jit(solution)/shard_map/psum | solution.py:85
  328.5 2.5 add_convert_fusion
  (14 shorter events, 0.1 us)
Async XLA Ops:
  6.5 1.0 copy-start
  6.5 12.1 %copy-start.5 = (bf16[32,128]{1,0:T(8,128)(2,1)S(1)}, bf16[32,128]{1,0:T(8,128)(2,1)}, u32[]{:S(2)}) copy-start(bf16[32,128]{1,0:T(8,128)(2,1)} %param.13) | copy-start | bytes 24580
  6.5 58.0 %all-gather.4.cloned.1.call-start = ((), (), s32[]{:S(2)}) async-start(), calls=%async_computation | async-start | bytes 5242880 | tf_op jit(solution)/shard_map/all_gather | solution.py:36
  10.0 138.8 %all-gather.6.cloned.1.call-start = ((), (), s32[]{:S(2)}) async-start(), calls=%async_computation.1 | async-start | bytes 6389760 | tf_op jit(solution)/shard_map/all_gather | solution.py:47
  10.8 214.9 %all-gather.8.cloned.1.call-start = ((), (), s32[]{:S(2)}) async-start(), calls=%async_computation.2 | async-start | bytes 2129920 | tf_op jit(solution)/shard_map/all_gather | solution.py:82
  11.5 317.0 %all-reduce.2.cloned.1.call-start = ((), (), s32[]{:S(2)}) async-start(), calls=%async_computation.3 | async-start | bytes 8388608 | tf_op jit(solution)/shard_map/psum | solution.py:85
  12.8 136.0 %copy-start.6 = (f32[2048]{0:T(1024)S(1)}, f32[2048]{0:T(1024)}, u32[]{:S(2)}) copy-start(f32[2048]{0:T(1024)} %param.10) | copy-start | bytes 24580
  159.4 3.7 %collective-permute-start = (bf16[6,3,512]{2,0,1:T(8,128)(2,1)S(1)}, bf16[6,3,512]{2,0,1:T(8,128)(2,1)S(1)}, u32[]{:S(2)}, u32[]{:S(2)}) collective-permute-start(bf16[6,3,512]{2,0,1:T(8,128)(2,1)S(1)} %slice.86), channel_id=1, source_target_pairs={{0,4},{4,8},{8,12},{12,16},{16,20},{20,24},{24,28},{28,32},{32,36}... | collective-permute-start | bytes 55304 | tf_op jit(solution)/shard_map/ppermute | solution.py:10
  168.7 2.7 copy-start.1
  171.7 5.5 %copy-start.3 = (bf16[1024,1,512]{2,0,1:T(8,128)(2,1)}, bf16[1024,1,512]{2,0,1:T(8,128)(2,1)S(1)}, u32[]{:S(2)}) copy-start(bf16[1024,1,512]{2,0,1:T(8,128)(2,1)S(1)} %fusion.20) | copy-start | bytes 3145732
  172.2 7.1 %copy-start.2 = (f32[1024,3,512]{2,0,1:T(8,128)S(1)}, f32[1024,3,512]{2,0,1:T(8,128)}, u32[]{:S(2)}) copy-start(f32[1024,3,512]{2,0,1:T(8,128)} %copy-done.1) | copy-start | bytes 18874372
  172.3 7.4 %collective-permute-start.1 = (bf16[128,512]{1,0:T(8,128)(2,1)S(1)}, bf16[128,512]{1,0:T(8,128)(2,1)S(1)}, u32[]{:S(2)}, u32[]{:S(2)}) collective-permute-start(bf16[128,512]{1,0:T(8,128)(2,1)S(1)} %slice_bitcast_fusion.1), channel_id=1, source_target_pairs={{0,4},{4,8},{8,12},{12,16},{16,20},{20,24},{24,28},{28,32},{32,36}... | collective-permute-start | bytes 393224 | tf_op jit(solution)/shard_map/ppermute | solution.py:10
  186.6 39.1 %copy-start.7 = (f32[512]{0:T(512)S(1)}, f32[512]{0:T(512)}, u32[]{:S(2)}) copy-start(f32[512]{0:T(512)} %param.14) | copy-start | bytes 6148
  189.8 138.7 %copy-start.4 = (bf16[1024,512]{1,0:T(8,128)(2,1)S(1)}, bf16[1024,512]{1,0:T(8,128)(2,1)}, u32[]{:S(2)}) copy-start(bf16[1024,512]{1,0:T(8,128)(2,1)} %fusion.24) | copy-start | bytes 3145732
Sparse Core Ops, SparseCore 0:
  10.1 54.3 all-gather.3
  67.4 81.3 all-gather.5
  151.6 74.0 all-gather.7
  233.4 94.9 all-reduce.1
where the time goes:
time: 338 us; the launch traced here: 337 us
  waiting for transfers between devices  255 us (75%)
  matrix products  35.6 us (11%)
  between operations  13.3 us (4%)
  other arithmetic  12.9 us (4%)
  local copies, waits for them, and re-layouts  12.7 us (4%)
  starting transfers between devices  7.53 us (2%)
    psum x1, waiting for transfers between devices, body(): summed = lax.psum(partials.astype(jnp.bfloat16), 'tp').astype(jnp.float32)  95.2 us
    all_gather x1, waiting for transfers between devices, body(): lax.all_gather(in_weight, 'seq', axis=0, tiled=True)  81.2 us
    all_gather x1, waiting for transfers between devices, body(): features = lax.all_gather(own_feats, 'tp', axis=1, tiled=True)  40.8 us
    all_gather x1, waiting for transfers between devices, body(): lax.all_gather(out_weight, 'seq', axis=1, tiled=True)  35.9 us
    dot_general x1, matrix products, body(): jnp.einsum('td,dsc->tsc', normed, lax.all_gather(in_weight, 'seq', axis=0...  10.5 us
    dot_general x1, matrix products, body(): jnp.dot(gated, lax.all_gather(out_weight, 'seq', axis=1, tiled=True), pre...  7.59 us
    ppermute x2, starting transfers between devices, from_behind(): return lax.ppermute(block, axis, route)  7.41 us
  transfers between devices with their start and end apart: 6, of which 5 were waited for; matrix products, arithmetic and copies ran while one was open for 13% of the time, Pallas kernels for 0%

commit v1 on v0

--- a/solution.py
+++ b/solution.py
@@ -2,6 +2,12 @@
 import jax.numpy as jnp
 from jax import lax
 from jax.sharding import PartitionSpec as P
+
+
+def summed_here(shard, axis):
+    parts = lax.all_gather(shard, axis, axis=0, tiled=False)
+    result = parts.sum(axis=0)
+    return result
 
 
 def from_behind(block, axis, distance):
@@ -82,7 +88,7 @@
         lax.all_gather(out_weight, "seq", axis=1, tiled=True),
         preferred_element_type=jnp.float32,
     )
-    summed = lax.psum(partials.astype(jnp.bfloat16), "tp").astype(jnp.float32)
+    summed = summed_here(partials.astype(jnp.bfloat16), "tp").astype(jnp.float32)
     own_share = lax.dynamic_slice_in_dim(summed, lax.axis_index("tp") * local_width, local_width, 1)
     return (own_feats.astype(jnp.float32) + own_share).astype(jnp.bfloat16)
 

time: 338 us -> 409 us (1.21)
  waiting for transfers between devices: 255 us -> 314 us
  other arithmetic: 12.9 us -> 25 us
    all_gather x0 -> x1, waiting for transfers between devices: none -> 154 us  [summed_here(): parts = lax.all_gather(shard, axis, axis=0, tiled=False)]
    psum x1 -> x0, waiting for transfers between devices: 95.2 us -> none  [body(): summed = lax.psum(partials.astype(jnp.bfloat16), 'tp').astype(jnp.float32)]
    reduce_sum x0 -> x1, other arithmetic: none -> 12 us  [summed_here(): result = parts.sum(axis=0)]
  transfers between devices with their start and end apart: 6 -> 6, of which waited for: 5 -> 5; matrix products, arithmetic and copies ran while one was open for 13% -> 11% of each run, Pallas kernels for 0% -> 0%
where the time goes in v1:
time: 409 us; the launch traced here: 408 us
  waiting for transfers between devices  314 us (77%)
  matrix products  35.5 us (9%)
  other arithmetic  25 us (6%)
  between operations  13.3 us (3%)
  local copies, waits for them, and re-layouts  12.8 us (3%)
  starting transfers between devices  7.51 us (2%)
    all_gather x1, waiting for transfers between devices, summed_here(): parts = lax.all_gather(shard, axis, axis=0, tiled=False)  154 us
    all_gather x1, waiting for transfers between devices, body(): lax.all_gather(in_weight, 'seq', axis=0, tiled=True)  81.2 us
    all_gather x1, waiting for transfers between devices, body(): features = lax.all_gather(own_feats, 'tp', axis=1, tiled=True)  40.9 us
    all_gather x1, waiting for transfers between devices, body(): lax.all_gather(out_weight, 'seq', axis=1, tiled=True)  35.8 us
    reduce_sum x1, other arithmetic, summed_here(): result = parts.sum(axis=0)  12 us
    dot_general x1, matrix products, body(): jnp.einsum('td,dsc->tsc', normed, lax.all_gather(in_weight, 'seq', axis=0...  10.5 us
  transfers between devices with their start and end apart: 6, of which 5 were waited for; matrix products, arithmetic and copies ran while one was open for 11% of the time, Pallas kernels for 0%

profile of v1, /device:TPU:1, one launch (start us, length us, event | category | flops | bytes accessed | tf_op | source)
XLA Modules:
  0.0 408.2 jit_solution(3148416070523768225)
XLA Ops:
  6.5 0.0 copy-start
  6.5 0.0 all-gather.6.cloned.1.call-start
  6.5 1.0 copy-done
  7.6 2.4 fusion.24
  10.0 0.0 all-gather.6.cloned.1.call-update
  10.0 0.0 all-gather.8.cloned.1.call-start
  10.1 0.7 all-gather.8.cloned.1.call-update
  10.8 0.0 all-gather.10.cloned.1.call-start
  10.8 0.7 all-gather.10.cloned.1.call-update
  11.5 0.0 all-gather.12.cloned.1.call-start
  11.6 1.2 fusion.38
  12.8 0.0 copy-start.7
  12.8 5.8 %fusion.3 = bf16[128,128,32]{1,2,0:T(8,128)(2,1)} fusion(s32[128,128]{1,0:T(8,128)S(1)} %iota_subtract_fusion, bf16[32,128]{1,0:T(8,128)(2,1)} %param.13), kind=kOutput, calls=%fused_computation.7 | convolution fusion | flops 136314880 | bytes 1122304 | tf_op jit(solution)/shard_map/isj,gj->gis/dot_general | solution.py:73
  18.6 0.0 copy-done.6
  18.6 5.1 %fusion.4 = bf16[128,128,32]{1,2,0:T(8,128)(2,1)} fusion(s32[128,128]{1,0:T(8,128)S(1)} %broadcast_add_fusion, bf16[32,128]{1,0:T(8,128)(2,1)S(1)} %copy-done.6), kind=kOutput, calls=%fused_computation.8 | convolution fusion | flops 136314880 | bytes 1122304 | tf_op jit(solution)/shard_map/isj,gj->gis/dot_general | solution.py:74
  23.7 40.9 %all-gather.6.cloned.1.call-done = bf16[1024,2048]{1,0:T(8,128)(2,1)} async-done(((bf16[1024,512]{1,0:T(8,128)(2,1)}), bf16[1024,2048]{1,0:T(8,128)(2,1)}) %all-gather.6.cloned.1.call-update) | async-done | bytes 4194320 | tf_op jit(solution)/shard_map/all_gather | solution.py:42
  64.6 3.1 fusion
  67.7 81.2 %all-gather.8.cloned.1.call-done = bf16[2048,3,512]{2,0,1:T(8,128)(2,1)} async-done(((bf16[32,3,512]{2,0,1:T(8,128)(2,1)}), bf16[2048,3,512]{2,0,1:T(8,128)(2,1)}) %all-gather.8.cloned.1.call-update) | async-done | bytes 6291472 | tf_op jit(solution)/shard_map/all_gather | solution.py:53
  148.9 0.0 copy-done.7
  148.9 10.5 %fusion.17 = bf16[1024,3,512]{2,0,1:T(8,128)(2,1)S(1)} fusion(bf16[2048,3,512]{2,0,1:T(8,128)(2,1)} %all-gather.8.cloned.1.call-done, bf16[1024,2048]{1,0:T(8,128)(2,1)} %all-gather.6.cloned.1.call-done, f32[2048]{0:T(1024)S(1)} %copy-done.7, f32[1024]{0:T(1024)S(1)} %add_rsqrt_fusion), kind=kOutput, calls=%fused_computation.31 | convolution fusion | flops 6452412416 | bytes 13643776 | tf_op jit(solution)/shard_map/td,dsc->tsc/dot_general | solution.py:50
  159.5 2.7 collective-permute-start
  162.2 0.9 collective-permute-done
  163.1 5.6 %multiply_add_fusion = f32[1024,3,512]{2,0,1:T(8,128)S(1)} fusion(bf16[1024,3,512]{2,0,1:T(8,128)(2,1)S(1)} %fusion.17, bf16[6,3,512]{2,0,1:T(8,128)(2,1)S(1)} %collective-permute-done, f32[3,512]{1,0:T(4,128)S(1)} %get-tuple-element.12, f32[3,512]{1,0:T(4,128)S(1)} %get-tuple-element.13, f32[3,512]{1,0:T(4,128)S(1)} %get-tuple-element.14, ...), kind=kLoop, calls=%fused_computation.14 | loop fusion | flops 59768832 | bytes 9498624 | tf_op jit(solution)/shard_map/add | solution.py:24
  168.7 0.0 copy-start.2
  168.8 2.7 copy-done.2
  171.4 0.4 fusion.20
  171.8 0.0 copy-start.4
  171.8 0.5 copy.12
  172.3 4.7 %collective-permute-start.1 = (bf16[128,512]{1,0:T(8,128)(2,1)S(1)}, bf16[128,512]{1,0:T(8,128)(2,1)S(1)}, u32[]{:S(2)}, u32[]{:S(2)}) collective-permute-start(bf16[128,512]{1,0:T(8,128)(2,1)S(1)} %slice_bitcast_fusion.1), channel_id=1, source_target_pairs={{0,4},{4,8},{8,12},{12,16},{16,20},{20,24},{24,28},{28,32},{32,36}... | collective-permute-start | bytes 393224 | tf_op jit(solution)/shard_map/ppermute | solution.py:16
  177.0 0.3 copy.29
  177.3 2.1 fusion.26
  179.4 0.4 fusion.42
  179.7 0.0 collective-permute-done.1
  179.8 1.1 pad_maximum_fusion.1
  180.8 2.3 copy.14
  183.1 1.5 copy.30
  184.6 2.1 add_bitcast_fusion
  186.7 0.0 copy-start.8
  186.7 0.9 copy.16
  187.6 0.5 copy.52
  188.0 1.9 copy.17
  189.9 35.8 %all-gather.10.cloned.1.call-done = bf16[512,2048]{0,1:T(8,128)(2,1)} async-done(((bf16[512,32]{0,1:T(8,128)(2,1)}), bf16[512,2048]{0,1:T(8,128)(2,1)}) %all-gather.10.cloned.1.call-update) | async-done | bytes 2097168 | tf_op jit(solution)/shard_map/all_gather | solution.py:88
  225.8 7.5 %convolution_convert_fusion = bf16[1024,2048]{1,0:T(8,128)(2,1)} fusion(bf16[512,2048]{0,1:T(8,128)(2,1)} %all-gather.10.cloned.1.call-done, f32[1024,3,512]{2,0,1:T(8,128)} %copy-done.2, f32[1024,512]{1,0:T(8,128)} %copy.17, f32[512]{0:T(512)S(1)} %copy-done.8, bf16[1024,1,512]{2,0,1:T(8,128)(2,1)} %copy-done.4), kind=kOutput, calls=%fused_computation.21 | convolution fusion | flops 2152202240 | bytes 11536384 | tf_op jit(solution)/shard_map/dot_general | solution.py:86
  233.3 0.0 all-gather.12.cloned.1.call-update
  233.3 153.8 %all-gather.12.cloned.1.call-done = bf16[4096,2048]{1,0:T(8,128)(2,1)} async-done(((bf16[1024,2048]{1,0:T(8,128)(2,1)}), bf16[4096,2048]{1,0:T(8,128)(2,1)}) %all-gather.12.cloned.1.call-update) | async-done | bytes 16777232 | tf_op jit(solution)/shard_map/all_gather | solution.py:8
  387.1 12.0 %reduce_sum.22 = bf16[1024,2048]{1,0:T(8,128)(2,1)} reduce(bf16[4,1024,2048]{2,1,0:T(8,128)(2,1)} %bitcast.78, bf16[]{:T(256)} %constant.7.clone.1), dimensions={0}, to_apply=%region_1.0 | reduce | flops 6291456 | bytes 20971522 | tf_op jit(solution)/shard_map/reduce_sum | solution.py:9
  399.1 0.0 copy-done.5
  399.1 2.5 add_convert_fusion
  (17 shorter events, 0.1 us)
Async XLA Ops:
  6.5 1.0 copy-start
  6.5 12.0 %copy-start.6 = (bf16[32,128]{1,0:T(8,128)(2,1)S(1)}, bf16[32,128]{1,0:T(8,128)(2,1)}, u32[]{:S(2)}) copy-start(bf16[32,128]{1,0:T(8,128)(2,1)} %param.13) | copy-start | bytes 24580
  6.5 58.1 %all-gather.6.cloned.1.call-start = ((), (), s32[]{:S(2)}) async-start(), calls=%async_computation | async-start | bytes 5242880 | tf_op jit(solution)/shard_map/all_gather | solution.py:42
  10.0 138.9 %all-gather.8.cloned.1.call-start = ((), (), s32[]{:S(2)}) async-start(), calls=%async_computation.1 | async-start | bytes 6389760 | tf_op jit(solution)/shard_map/all_gather | solution.py:53
  10.8 215.0 %all-gather.10.cloned.1.call-start = ((), (), s32[]{:S(2)}) async-start(), calls=%async_computation.2 | async-start | bytes 2129920 | tf_op jit(solution)/shard_map/all_gather | solution.py:88
  11.5 375.6 %all-gather.12.cloned.1.call-start = ((), (), s32[]{:S(2)}) async-start(), calls=%async_computation.3 | async-start | bytes 20971520 | tf_op jit(solution)/shard_map/all_gather | solution.py:8
  12.8 136.1 %copy-start.7 = (f32[2048]{0:T(1024)S(1)}, f32[2048]{0:T(1024)}, u32[]{:S(2)}) copy-start(f32[2048]{0:T(1024)} %param.10) | copy-start | bytes 24580
  159.5 3.7 collective-permute-start
  168.7 2.7 copy-start.2
  171.8 5.5 %copy-start.4 = (bf16[1024,1,512]{2,0,1:T(8,128)(2,1)}, bf16[1024,1,512]{2,0,1:T(8,128)(2,1)S(1)}, u32[]{:S(2)}) copy-start(bf16[1024,1,512]{2,0,1:T(8,128)(2,1)S(1)} %fusion.20) | copy-start | bytes 3145732
  172.3 7.1 %copy-start.3 = (f32[1024,3,512]{2,0,1:T(8,128)S(1)}, f32[1024,3,512]{2,0,1:T(8,128)}, u32[]{:S(2)}) copy-start(f32[1024,3,512]{2,0,1:T(8,128)} %copy-done.2) | copy-start | bytes 18874372
  172.3 7.4 %collective-permute-start.1 = (bf16[128,512]{1,0:T(8,128)(2,1)S(1)}, bf16[128,512]{1,0:T(8,128)(2,1)S(1)}, u32[]{:S(2)}, u32[]{:S(2)}) collective-permute-start(bf16[128,512]{1,0:T(8,128)(2,1)S(1)} %slice_bitcast_fusion.1), channel_id=1, source_target_pairs={{0,4},{4,8},{8,12},{12,16},{16,20},{20,24},{24,28},{28,32},{32,36}... | collective-permute-start | bytes 393224 | tf_op jit(solution)/shard_map/ppermute | solution.py:16
  186.7 39.1 %copy-start.8 = (f32[512]{0:T(512)S(1)}, f32[512]{0:T(512)}, u32[]{:S(2)}) copy-start(f32[512]{0:T(512)} %param.14) | copy-start | bytes 6148
  387.1 12.0 %copy-start.5 = (bf16[1024,512]{1,0:T(8,128)(2,1)S(1)}, bf16[1024,512]{1,0:T(8,128)(2,1)}, u32[]{:S(2)}) copy-start(bf16[1024,512]{1,0:T(8,128)(2,1)} %fusion.24) | copy-start | bytes 3145732
  387.1 14.5 %copy-start.1 = (bf16[512,512]{1,0:T(8,128)(2,1)S(1)}, bf16[512,512]{1,0:T(8,128)(2,1)}, u32[]{:S(2)}) copy-start(bf16[512,512]{1,0:T(8,128)(2,1)} %param.9) | copy-start | bytes 1572868
Sparse Core Ops, SparseCore 0:
  10.1 54.4 all-gather.5
  67.4 81.4 all-gather.7
  151.7 74.0 all-gather.9
  233.4 153.6 all-gather.11
